TPU v7x, 32 devices: a whole 2x2x4 slice. The times are simulated.
32 devices in a mesh: conf: 2 (over x), virt: 16 (over z, y, core).
Axes of the slice: x: 2, y: 2, z: 4, core: 2. Of those that a mesh axis runs over, the one named last changes fastest.
Arguments:
- i_factors: float32 [32, 1024, 2048], P('conf', 'virt'), parts along dimension 0, may hold values from -0.6 to 0.6
- j_factors: float32 [4, 1024, 2048], P('conf', 'virt'), parts along dimension 0, may hold values from -0.6 to 0.6
- occ_i: float32 [32], P('conf'), parts along dimension 0, may hold values from -2 to -0.3
- occ_j: float32 [4], P('conf'), parts along dimension 0, may hold values from -2 to -0.3
- virt_energy: float32 [2048], P(('conf', 'virt')), parts along dimension 0, may hold values from 0.3 to 3
Outputs:
- density: float32 [32, 1024, 2048], P('conf', 'virt'), parts along dimension 0
There are 2 independent parts, one for each index of `conf`. A program takes and returns all parts, laid end to end along the dimension named above; each array names one. Nothing has to cross between parts.
All inputs are finite; a program needn't handle non-finite values.
Results may differ from a plain program's by a relative error of at most 0.00005.
Values sent between devices are 32-bit elements; how exact they have to be, the bound alone decides.
A program may use at most 128 MiB of HBM per device.

v0:
```python
import functools

import jax
import jax.numpy as jnp
from jax import lax
from jax.experimental import pallas as pl
from jax.experimental.pallas import tpu as pltpu
from jax.sharding import PartitionSpec as P

LANES = 128
MESH = pl.DeviceIdType.MESH


def split(value):
    high = value.astype(jnp.bfloat16)
    low = (value - high.astype(jnp.float32)).astype(jnp.bfloat16)
    return high, low


def kernel(
    n, columns, i_ref, j_ref, energy_ref, occ_i_ref, occ_j_ref, part_ref, amp_ref, last_j_ref,
    i_high, i_low, j_all, direct, x_send, x_recv, total, j_parts, amp_parts, row_ref,
    local_sem, j_send_sem, j_recv_sem, x_send_sem, x_recv_sem, amp_sem,
):
    levels = n // 2 // columns
    me = lax.axis_index("virt")
    core = lax.rem(me, 2)
    chip = me // 2
    y = lax.rem(chip, columns)
    z = chip // columns
    rows, depth = i_ref.shape
    pair = 2 * LANES
    tall = 256
    wide = 512

    load_i = pltpu.make_async_copy(i_ref, total, local_sem.at[0])
    load_i.start()
    load_j = pltpu.make_async_copy(j_ref, j_all.at[me], local_sem.at[1])
    load_j.start()

    barrier = pltpu.get_barrier_semaphore()

    @pl.loop(1, n)
    def _(step):
        pl.semaphore_signal(
            barrier, inc=1, device_id={"virt": lax.rem(me + step, n)}, device_id_type=MESH
        )

    pl.semaphore_wait(barrier, n - 1)

    def j_copy(origin, way, device):
        return pltpu.make_async_remote_copy(
            src_ref=j_all.at[origin],
            dst_ref=j_all.at[origin],
            send_sem=j_send_sem.at[origin, way],
            recv_sem=j_recv_sem.at[origin],
            device_id={"virt": device},
            device_id_type=MESH,
        )

    def j_targets(origin, act):
        place = origin // 2
        same_core = lax.rem(origin, 2) == core
        in_column = jnp.logical_and(same_core, lax.rem(place, columns) == y)
        from_z = place // columns

        @pl.when(jnp.logical_and(in_column, jnp.logical_and(z >= from_z, z + 1 < levels)))
        def _():
            act(j_copy(origin, 0, me + 2 * columns))

        @pl.when(jnp.logical_and(in_column, jnp.logical_and(z <= from_z, z > 0)))
        def _():
            act(j_copy(origin, 1, me - 2 * columns))

        if columns == 2:
            @pl.when(in_column)
            def _():
                act(j_copy(origin, 2, me + 2 * (1 - 2 * y)))

        @pl.when(same_core)
        def _():
            act(j_copy(origin, 3, me + 1 - 2 * core))

    def x_copy(other):
        return pltpu.make_async_remote_copy(
            src_ref=x_send.at[other, pl.ds(0, rows + 1)],
            dst_ref=x_recv.at[me, pl.ds(0, rows + 1)],
            send_sem=x_send_sem.at[other],
            recv_sem=x_recv_sem.at[me],
            device_id={"virt": other},
            device_id_type=MESH,
        )

    def x_arrival(other):
        return pltpu.make_async_remote_copy(
            src_ref=x_send.at[other, pl.ds(0, rows + 1)],
            dst_ref=x_recv.at[other, pl.ds(0, rows + 1)],
            send_sem=x_send_sem.at[other],
            recv_sem=x_recv_sem.at[other],
            device_id={"virt": other},
            device_id_type=MESH,
        )

    def x_stay():
        return pltpu.make_async_copy(x_send.at[me], x_recv.at[me], local_sem.at[2])

    load_j.wait()
    j_targets(me, lambda copy: copy.start())
    load_i.wait()

    @pl.loop(0, rows // 32)
    def _(step):
        part = pl.ds(pl.multiple_of(step * 32, 32), 32)
        high, low = split(total[part, :])
        i_high[part, :] = high
        i_low[part, :] = low
        total[part, :] = jnp.zeros((32, depth), jnp.float32)

    width = energy_ref.shape[1]
    energy = energy_ref[...]
    twice = jnp.concatenate([energy, energy], axis=1)
    tall_energy = jnp.broadcast_to(twice, (LANES, LANES)).T[:width]
    for orbital in range(rows // width):
        row_ref[orbital * width:(orbital + 1) * width, :] = tall_energy - occ_i_ref[orbital]
    col_lane = lax.broadcasted_iota(jnp.int32, (8, LANES), 1)
    col_term = jnp.broadcast_to(twice, (8, LANES)) - jnp.where(
        col_lane < width, occ_j_ref[0], occ_j_ref[1]
    )

    @pl.loop(0, n)
    def _(other):
        x_send[other, pl.ds(rows, 8), :] = col_term

    def split_j(place, copies):
        per = LANES // 32

        @pl.loop(0, 2 * per)
        def _(step):
            from_rows = pl.ds(pl.multiple_of(lax.rem(step, per) * 32, 32), 32)
            high, low = split(j_all[2 * place + step // per, from_rows, :])
            base = pl.multiple_of(step * 32, 32)
            j_parts[pl.ds(base, 32), :] = high
            j_parts[pl.ds(pair + base, 32), :] = low
            if copies == 3:
                j_parts[pl.ds(2 * pair + base, 32), :] = high

    toward = jnp.where(2 * z >= levels, -1, 1)

    def visit(step):
        level = step // 4
        kind = lax.rem(step // 2, 2)
        sign = lax.rem(step, 2)
        distance = level - kind
        at_y = jnp.where(kind == 0, y, columns - 1 - y)

        def on(way):
            at_z = z + toward * (1 - 2 * way) * distance
            valid = jnp.logical_and(distance >= 0, jnp.logical_and(at_z >= 0, at_z < levels))
            valid = jnp.logical_and(valid, jnp.logical_or(distance > 0, way == 0))
            if columns == 1:
                valid = jnp.logical_and(valid, kind == 0)
            return valid, at_z * columns + at_y

        return on, sign

    visits = 4 * (levels + columns - 1)

    @pl.loop(0, visits)
    def _(step):
        on, sign = visit(step)

        @pl.when(sign == 0)
        def _():
            for way in range(2):
                valid, place = on(way)
                origin = 2 * place + core

                @pl.when(jnp.logical_and(valid, origin != me))
                def _():
                    j_copy(origin, 0, me).wait_recv()
                    j_targets(origin, lambda copy: copy.start())

        valid, place = on(sign)

        @pl.when(valid)
        def _():
            j_copy(2 * place + 1 - core, 0, me).wait_recv()
            split_j(place, 2)
            lane = lax.broadcasted_iota(jnp.int32, (LANES // 2, LANES), 1)
            half = LANES // 2
            contract = (((1,), (1,)), ((), ()))

            @pl.loop(0, rows // tall)
            def _(block):
                start = pl.multiple_of(block * tall, tall)
                high, low = i_high[pl.ds(start, tall), :], i_low[pl.ds(start, tall), :]
                j_high, j_low = j_parts[pl.ds(0, pair), :], j_parts[pl.ds(pair, pair), :]
                dot = functools.partial(
                    lax.dot_general, dimension_numbers=contract,
                    preferred_element_type=jnp.float32,
                )
                block_pair = dot(high, j_high) + (dot(high, j_low) + dot(low, j_high))
                direct[place, pl.ds(start, tall), :] = block_pair
                for side in range(2):
                    for group in range(tall // LANES):
                        tile = block_pair[
                            group * LANES:(group + 1) * LANES, side * LANES:(side + 1) * LANES
                        ]
                        turned = tile.T
                        moved = pltpu.roll(turned, half, 1)
                        first = jnp.where(lane < half, turned[:half], moved[half:])
                        second = jnp.where(lane < half, moved[:half], turned[half:])
                        base = start + group * LANES
                        x_send[2 * place + side, pl.ds(base, half), :] = first
                        x_send[2 * place + side, pl.ds(base + half, half), :] = second

            for side in range(2):
                other = 2 * place + side

                @pl.when(other != me)
                def _():
                    x_copy(other).start()

                @pl.when(other == me)
                def _():
                    x_stay().start()

    def await_blocks(place):
        for side in range(2):
            other = 2 * place + side

            @pl.when(other != me)
            def _():
                x_arrival(other).wait_recv()

            @pl.when(other == me)
            def _():
                x_stay().wait()

    def amplitudes(place, part):
        for side in range(2):
            other = 2 * place + side
            lanes = slice(side * LANES, (side + 1) * LANES)
            swapped = x_recv[other, part, :]
            own = direct[place, part, lanes]
            denominator = row_ref[part, :] + x_recv[other, pl.ds(rows, 1), :]
            high, low = split((swapped - 2.0 * own) / denominator)
            amp_parts[part, side * LANES:(side + 1) * LANES] = high
            amp_parts[part, pair + side * LANES:pair + (side + 1) * LANES] = high
            amp_parts[part, 2 * pair + side * LANES:2 * pair + (side + 1) * LANES] = low

    farthest = jnp.maximum(z, levels - 1 - z)
    back = z - toward * farthest
    forth = z + toward * farthest
    back_valid = jnp.logical_and(back >= 0, back < levels)
    last_place = jnp.where(back_valid, back, forth) * columns + columns - 1 - y

    @pl.loop(0, visits)
    def _(step):
        on, sign = visit(step)
        valid, place = on(sign)

        @pl.when(jnp.logical_and(valid, place != last_place))
        def _():
            split_j(place, 3)
            await_blocks(place)

            @pl.loop(0, rows // tall)
            def _(block):
                amplitudes(place, pl.ds(pl.multiple_of(block * tall, tall), tall))

            @pl.loop(0, depth // pair)
            def _(strip):
                at = pl.ds(pl.multiple_of(strip * pair, pair), pair)
                total[:, at] += jnp.dot(
                    amp_parts[...], j_parts[:, at], preferred_element_type=jnp.float32
                )

    store = pltpu.make_async_copy(total, part_ref, local_sem.at[0])
    store.start()
    split_j(last_place, 3)
    store_j = pltpu.make_async_copy(j_parts, last_j_ref, local_sem.at[1])
    store_j.start()

    @pl.loop(0, n)
    def _(other):
        j_targets(other, lambda copy: copy.wait_send())

    await_blocks(last_place)

    def store_amp(block):
        part = pl.ds(pl.multiple_of(block * tall, tall), tall)
        return pltpu.make_async_copy(amp_parts.at[part], amp_ref.at[part], amp_sem.at[block])

    @pl.loop(0, rows // tall)
    def _(block):
        amplitudes(last_place, pl.ds(pl.multiple_of(block * tall, tall), tall))
        store_amp(block).start()

    @pl.loop(0, n)
    def _(other):
        @pl.when(other != me)
        def _():
            x_copy(other).wait_send()

    store.wait()
    store_j.wait()

    @pl.loop(0, rows // tall)
    def _(block):
        store_amp(block).wait()


def finish(part_ref, amp_ref, j_ref, out_ref):
    wide = 256
    for start in range(0, part_ref.shape[1], wide):
        at = slice(start, start + wide)
        out_ref[:, at] = part_ref[:, at] + jnp.dot(
            amp_ref[...], j_ref[:, at], preferred_element_type=jnp.float32
        )


def fused(columns, i_factors, j_factors, occ_i, occ_j, virt_energy):
    n = lax.axis_size("virt")
    ni, width, depth = i_factors.shape
    nj = j_factors.shape[0]
    rows = ni * width
    anywhere = pl.BlockSpec(memory_space=pl.ANY)
    vmem = pl.BlockSpec(memory_space=pltpu.VMEM)
    f32, bf16 = jnp.float32, jnp.bfloat16
    dma = pltpu.SemaphoreType.DMA
    smem = pl.BlockSpec(memory_space=pltpu.SMEM)
    part, amp, last_j = pl.pallas_call(
        functools.partial(kernel, n, columns),
        out_shape=(
            jax.ShapeDtypeStruct((rows, depth), f32),
            jax.ShapeDtypeStruct((rows, 6 * LANES), bf16),
            jax.ShapeDtypeStruct((6 * LANES, depth), bf16),
        ),
        in_specs=[anywhere, anywhere, vmem, smem, smem],
        out_specs=(anywhere, anywhere, anywhere),
        scratch_shapes=[
            pltpu.VMEM((rows, depth), bf16),
            pltpu.VMEM((rows, depth), bf16),
            pltpu.VMEM((n, LANES, depth), f32),
            pltpu.VMEM((n // 2, rows, 2 * LANES), f32),
            pltpu.VMEM((n, rows + 8, LANES), f32),
            pltpu.VMEM((n, rows + 8, LANES), f32),
            pltpu.VMEM((rows, depth), f32),
            pltpu.VMEM((6 * LANES, depth), bf16),
            pltpu.VMEM((rows, 6 * LANES), bf16),
            pltpu.VMEM((rows, LANES), f32),
            dma((3,)),
            dma((n, 4)),
            dma((n,)),
            dma((n,)),
            dma((n,)),
            dma((rows // 256,)),
        ],
        compiler_params=pltpu.CompilerParams(
            collective_id=0, has_side_effects=True, vmem_limit_bytes=67043328
        ),
        name="pair_exchange",
    )(
        i_factors.reshape(rows, depth), j_factors.reshape(nj * width, depth),
        virt_energy.reshape(1, width), occ_i, occ_j,
    )
    tall = 256
    out = pl.pallas_call(
        finish,
        out_shape=jax.ShapeDtypeStruct((rows, depth), f32),
        grid=(rows // tall,),
        in_specs=[
            pl.BlockSpec((tall, depth), lambda step: (step, 0)),
            pl.BlockSpec((tall, 6 * LANES), lambda step: (step, 0)),
            pl.BlockSpec((6 * LANES, depth), lambda step: (0, 0)),
        ],
        out_specs=pl.BlockSpec((tall, depth), lambda step: (step, 0)),
        name="last_block",
    )(part, amp, last_j)
    return out.reshape(i_factors.shape)


def transpose_blocks(pair_block, blocks):
    leading = pair_block.shape[:-2]
    height = pair_block.shape[-2]
    width = pair_block.shape[-1]
    parts = pair_block.reshape(leading + (height, blocks, height))
    moved = jnp.swapaxes(parts, -1, -3)
    return moved.reshape(leading + (height, width))


def general(i_factors, j_factors, occ_i, occ_j, virt_energy):
    blocks = lax.axis_size("virt")
    left_rows = i_factors.reshape(-1, i_factors.shape[2])
    density = jnp.zeros(i_factors.shape, jnp.float32)
    whole_energy = lax.all_gather(virt_energy, "virt", axis=0, tiled=True)
    for index in range(j_factors.shape[0]):
        whole_rows = lax.all_gather(j_factors[index], "virt", axis=0, tiled=True)
        pair_block = jnp.dot(left_rows, whole_rows.T, precision=lax.Precision.HIGHEST)
        pair_block = pair_block.reshape(i_factors.shape[0], i_factors.shape[1], whole_rows.shape[0])
        swapped = lax.all_to_all(
            transpose_blocks(pair_block, blocks), "virt", split_axis=2, concat_axis=2, tiled=True
        )
        denominator = (
            virt_energy[None, :, None]
            + whole_energy[None, None, :]
            - occ_i[:, None, None]
            - occ_j[index]
        )
        amplitude = (swapped - 2.0 * pair_block) / denominator
        density = density + jnp.einsum(
            "iab,bp->iap", amplitude, whole_rows, precision=lax.Precision.HIGHEST
        )
    return density


def chip_columns(mesh):
    group = list(mesh.devices.reshape(-1, mesh.shape["virt"])[0])
    if len(group) % 2:
        return 0
    chips = group[::2]
    heights = len({getattr(device, "coords", (0, 0, place))[2] for place, device in enumerate(chips)})
    columns, left = divmod(len(chips), heights)
    return columns if left == 0 and columns in (1, 2) else 0


def body(columns, i_factors, j_factors, occ_i, occ_j, virt_energy):
    ni, width, depth = i_factors.shape
    nj = j_factors.shape[0]
    fits = nj == 2 and nj * width == LANES and (ni * width) % 256 == 0 and depth % 512 == 0
    n = lax.axis_size("virt")
    room = 4 * ni * width * depth * 2 + 4 * n * LANES * (depth + 3 * (ni * width + 8))
    if columns and fits and room < 58 * 2**20:
        return fused(columns, i_factors, j_factors, occ_i, occ_j, virt_energy)
    return general(i_factors, j_factors, occ_i, occ_j, virt_energy)


def solution(mesh):
    placed = (
        P("conf", "virt", None),
        P("conf", "virt", None),
        P("conf"),
        P("conf"),
        P(("conf", "virt")),
    )
    return jax.shard_map(
        functools.partial(body, chip_columns(mesh)),
        mesh=mesh, in_specs=placed, out_specs=P("conf", "virt", None), check_vma=False,
    )
```

profile of v0, /device:TPU:1, one launch (start us, length us, event | category | flops | bytes accessed | tf_op | source)
XLA Modules:
  0.0 257.3 jit_solution(16096290307146614693)
XLA Ops:
  0.0 247.2 %pair_exchange.1 = (f32[1024,2048]{1,0:T(8,128)}, bf16[1024,768]{1,0:T(8,128)(2,1)}, bf16[768,2048]{1,0:T(8,128)(2,1)}) custom-call(f32[1024,2048]{1,0:T(8,128)} %bitcast.4, f32[128,2048]{1,0:T(8,128)} %bitcast.5, f32[1,64]{1,0:T(1,128)} %bitcast.6, f32[16]{0:T(128)} %occ_i_ref.1, f32[2]{0:T(128)} %occ_j_ref.1), custom_call_target="tpu_custom_call" | custom-call | tf_op jit(solution)/shard_map/pair_exchange/pallas_call | solution.py:333
  247.2 10.1 %last_block.1 = f32[1024,2048]{1,0:T(8,128)} custom-call(f32[1024,2048]{1,0:T(8,128)} %get-tuple-element.8.part_ref, bf16[1024,768]{1,0:T(8,128)(2,1)} %get-tuple-element.9.amp_ref, bf16[768,2048]{1,0:T(8,128)(2,1)} %get-tuple-element.10.j_ref), custom_call_target="tpu_custom_call" | custom-call | tf_op jit(solution)/shard_map/last_block/pallas_call | solution.py:369
where the time goes:
time: 257 us
  Pallas kernels  257 us (100%)
    pallas_call x1, Pallas kernels, fused(): pl.pallas_call(functools.partial(kernel, n, columns), out_shape=(jax.Shap...  247 us
    pallas_call x1, Pallas kernels, fused(): pl.pallas_call(finish, out_shape=jax.ShapeDtypeStruct((rows, depth), f32)...  10.1 us

commit v1 on v0

--- a/solution.py
+++ b/solution.py
@@ -18,9 +18,9 @@
 
 
 def kernel(
-    n, columns, i_ref, j_ref, energy_ref, occ_i_ref, occ_j_ref, part_ref, amp_ref, last_j_ref,
-    i_high, i_low, j_all, direct, x_send, x_recv, total, j_parts, amp_parts, row_ref,
-    local_sem, j_send_sem, j_recv_sem, x_send_sem, x_recv_sem, amp_sem,
+    n, columns, i_ref, j_ref, energy_ref, occ_i_ref, occ_j_ref, total,
+    i_high, i_low, j_all, direct, x_send, x_recv, j_parts, amp_parts, row_ref,
+    local_sem, j_send_sem, j_recv_sem, x_send_sem, x_recv_sem,
 ):
     levels = n // 2 // columns
     me = lax.axis_index("virt")
@@ -31,7 +31,7 @@
     rows, depth = i_ref.shape
     pair = 2 * LANES
     tall = 256
-    wide = 512
+    chunks = rows // tall
 
     load_i = pltpu.make_async_copy(i_ref, total, local_sem.at[0])
     load_i.start()
@@ -40,13 +40,23 @@
 
     barrier = pltpu.get_barrier_semaphore()
 
-    @pl.loop(1, n)
-    def _(step):
-        pl.semaphore_signal(
-            barrier, inc=1, device_id={"virt": lax.rem(me + step, n)}, device_id_type=MESH
-        )
-
-    pl.semaphore_wait(barrier, n - 1)
+    def greet(device):
+        pl.semaphore_signal(barrier, inc=1, device_id={"virt": device}, device_id_type=MESH)
+
+    greet(me + 1 - 2 * core)
+    if columns == 2:
+        greet(me + 2 * (1 - 2 * y))
+
+    @pl.when(z + 1 < levels)
+    def _():
+        greet(me + 2 * columns)
+
+    @pl.when(z > 0)
+    def _():
+        greet(me - 2 * columns)
+
+    inner = jnp.logical_and(z > 0, z + 1 < levels).astype(jnp.int32)
+    pl.semaphore_wait(barrier, columns + (inner + 1 if levels > 1 else 0))
 
     def j_copy(origin, way, device):
         return pltpu.make_async_remote_copy(
@@ -81,25 +91,24 @@
         def _():
             act(j_copy(origin, 3, me + 1 - 2 * core))
 
-    def x_copy(other):
+    def x_rows(chunk):
+        return pl.ds(pl.multiple_of(chunk * tall, tall), tall)
+
+    def x_copy(other, origin, part, slot):
         return pltpu.make_async_remote_copy(
-            src_ref=x_send.at[other, pl.ds(0, rows + 1)],
-            dst_ref=x_recv.at[me, pl.ds(0, rows + 1)],
-            send_sem=x_send_sem.at[other],
-            recv_sem=x_recv_sem.at[me],
+            src_ref=x_send.at[other, part],
+            dst_ref=x_recv.at[origin, part],
+            send_sem=x_send_sem.at[other, slot],
+            recv_sem=x_recv_sem.at[origin, slot],
             device_id={"virt": other},
             device_id_type=MESH,
         )
 
-    def x_arrival(other):
-        return pltpu.make_async_remote_copy(
-            src_ref=x_send.at[other, pl.ds(0, rows + 1)],
-            dst_ref=x_recv.at[other, pl.ds(0, rows + 1)],
-            send_sem=x_send_sem.at[other],
-            recv_sem=x_recv_sem.at[other],
-            device_id={"virt": other},
-            device_id_type=MESH,
-        )
+    def x_block(other, origin, chunk):
+        return x_copy(other, origin, x_rows(chunk), chunk)
+
+    def x_energy(other, origin):
+        return x_copy(other, origin, pl.ds(rows, 1), chunks)
 
     def x_stay():
         return pltpu.make_async_copy(x_send.at[me], x_recv.at[me], local_sem.at[2])
@@ -185,6 +194,13 @@
         @pl.when(valid)
         def _():
             j_copy(2 * place + 1 - core, 0, me).wait_recv()
+            for side in range(2):
+                other = 2 * place + side
+
+                @pl.when(other != me)
+                def _():
+                    x_energy(other, me).start()
+
             split_j(place, 2)
             lane = lax.broadcasted_iota(jnp.int32, (LANES // 2, LANES), 1)
             half = LANES // 2
@@ -213,29 +229,39 @@
                         base = start + group * LANES
                         x_send[2 * place + side, pl.ds(base, half), :] = first
                         x_send[2 * place + side, pl.ds(base + half, half), :] = second
+                for side in range(2):
+                    other = 2 * place + side
+
+                    @pl.when(other != me)
+                    def _():
+                        x_block(other, me, block).start()
 
             for side in range(2):
                 other = 2 * place + side
-
-                @pl.when(other != me)
-                def _():
-                    x_copy(other).start()
 
                 @pl.when(other == me)
                 def _():
                     x_stay().start()
 
-    def await_blocks(place):
+    def await_energies(place):
         for side in range(2):
             other = 2 * place + side
 
             @pl.when(other != me)
             def _():
-                x_arrival(other).wait_recv()
+                x_energy(other, other).wait_recv()
 
             @pl.when(other == me)
             def _():
                 x_stay().wait()
+
+    def await_blocks(place, chunk):
+        for side in range(2):
+            other = 2 * place + side
+
+            @pl.when(other != me)
+            def _():
+                x_block(other, other, chunk).wait_recv()
 
     def amplitudes(place, part):
         for side in range(2):
@@ -250,6 +276,8 @@
             amp_parts[part, 2 * pair + side * LANES:2 * pair + (side + 1) * LANES] = low
 
     farthest = jnp.maximum(z, levels - 1 - z)
+    if columns == 2 and levels > 1:
+        farthest = jnp.where(farthest == levels - 1, farthest - 1, farthest)
     back = z - toward * farthest
     forth = z + toward * farthest
     back_valid = jnp.logical_and(back >= 0, back < levels)
@@ -263,11 +291,12 @@
         @pl.when(jnp.logical_and(valid, place != last_place))
         def _():
             split_j(place, 3)
-            await_blocks(place)
-
-            @pl.loop(0, rows // tall)
+            await_energies(place)
+
+            @pl.loop(0, chunks)
             def _(block):
-                amplitudes(place, pl.ds(pl.multiple_of(block * tall, tall), tall))
+                await_blocks(place, block)
+                amplitudes(place, x_rows(block))
 
             @pl.loop(0, depth // pair)
             def _(strip):
@@ -276,48 +305,36 @@
                     amp_parts[...], j_parts[:, at], preferred_element_type=jnp.float32
                 )
 
-    store = pltpu.make_async_copy(total, part_ref, local_sem.at[0])
-    store.start()
     split_j(last_place, 3)
-    store_j = pltpu.make_async_copy(j_parts, last_j_ref, local_sem.at[1])
-    store_j.start()
 
     @pl.loop(0, n)
     def _(other):
         j_targets(other, lambda copy: copy.wait_send())
 
-    await_blocks(last_place)
-
-    def store_amp(block):
-        part = pl.ds(pl.multiple_of(block * tall, tall), tall)
-        return pltpu.make_async_copy(amp_parts.at[part], amp_ref.at[part], amp_sem.at[block])
-
-    @pl.loop(0, rows // tall)
+    await_energies(last_place)
+
+    @pl.loop(0, chunks)
     def _(block):
-        amplitudes(last_place, pl.ds(pl.multiple_of(block * tall, tall), tall))
-        store_amp(block).start()
+        part = x_rows(block)
+        await_blocks(last_place, block)
+        amplitudes(last_place, part)
+
+        @pl.loop(0, depth // pair)
+        def _(strip):
+            at = pl.ds(pl.multiple_of(strip * pair, pair), pair)
+            total[part, at] += jnp.dot(
+                amp_parts[part, :], j_parts[:, at], preferred_element_type=jnp.float32
+            )
 
     @pl.loop(0, n)
     def _(other):
         @pl.when(other != me)
         def _():
-            x_copy(other).wait_send()
-
-    store.wait()
-    store_j.wait()
-
-    @pl.loop(0, rows // tall)
-    def _(block):
-        store_amp(block).wait()
-
-
-def finish(part_ref, amp_ref, j_ref, out_ref):
-    wide = 256
-    for start in range(0, part_ref.shape[1], wide):
-        at = slice(start, start + wide)
-        out_ref[:, at] = part_ref[:, at] + jnp.dot(
-            amp_ref[...], j_ref[:, at], preferred_element_type=jnp.float32
-        )
+            x_energy(other, me).wait_send()
+
+            @pl.loop(0, chunks)
+            def _(chunk):
+                x_block(other, me, chunk).wait_send()
 
 
 def fused(columns, i_factors, j_factors, occ_i, occ_j, virt_energy):
@@ -330,15 +347,11 @@
     f32, bf16 = jnp.float32, jnp.bfloat16
     dma = pltpu.SemaphoreType.DMA
     smem = pl.BlockSpec(memory_space=pltpu.SMEM)
-    part, amp, last_j = pl.pallas_call(
+    total = pl.pallas_call(
         functools.partial(kernel, n, columns),
-        out_shape=(
-            jax.ShapeDtypeStruct((rows, depth), f32),
-            jax.ShapeDtypeStruct((rows, 6 * LANES), bf16),
-            jax.ShapeDtypeStruct((6 * LANES, depth), bf16),
-        ),
+        out_shape=pltpu.VMEM((rows, depth), f32),
         in_specs=[anywhere, anywhere, vmem, smem, smem],
-        out_specs=(anywhere, anywhere, anywhere),
+        out_specs=vmem,
         scratch_shapes=[
             pltpu.VMEM((rows, depth), bf16),
             pltpu.VMEM((rows, depth), bf16),
@@ -346,39 +359,24 @@
             pltpu.VMEM((n // 2, rows, 2 * LANES), f32),
             pltpu.VMEM((n, rows + 8, LANES), f32),
             pltpu.VMEM((n, rows + 8, LANES), f32),
-            pltpu.VMEM((rows, depth), f32),
             pltpu.VMEM((6 * LANES, depth), bf16),
             pltpu.VMEM((rows, 6 * LANES), bf16),
             pltpu.VMEM((rows, LANES), f32),
             dma((3,)),
             dma((n, 4)),
             dma((n,)),
-            dma((n,)),
-            dma((n,)),
-            dma((rows // 256,)),
+            dma((n, rows // 256 + 1)),
+            dma((n, rows // 256 + 1)),
         ],
         compiler_params=pltpu.CompilerParams(
-            collective_id=0, has_side_effects=True, vmem_limit_bytes=67043328
+            collective_id=0, has_side_effects=True, vmem_limit_bytes=55 * 2**20
         ),
         name="pair_exchange",
     )(
         i_factors.reshape(rows, depth), j_factors.reshape(nj * width, depth),
         virt_energy.reshape(1, width), occ_i, occ_j,
     )
-    tall = 256
-    out = pl.pallas_call(
-        finish,
-        out_shape=jax.ShapeDtypeStruct((rows, depth), f32),
-        grid=(rows // tall,),
-        in_specs=[
-            pl.BlockSpec((tall, depth), lambda step: (step, 0)),
-            pl.BlockSpec((tall, 6 * LANES), lambda step: (step, 0)),
-            pl.BlockSpec((6 * LANES, depth), lambda step: (0, 0)),
-        ],
-        out_specs=pl.BlockSpec((tall, depth), lambda step: (step, 0)),
-        name="last_block",
-    )(part, amp, last_j)
-    return out.reshape(i_factors.shape)
+    return total.reshape(i_factors.shape)
 
 
 def transpose_blocks(pair_block, blocks):

time: 257 us -> 245 us (0.953)
  the two profiles are of different devices: /device:TPU:1 before, /device:TPU:9 now
where the time goes in v1:
time: 245 us; the launch traced here: 241 us
  Pallas kernels  237 us (97%)
  local copies, waits for them, and re-layouts  3.4 us (1%)
    pallas_call x1, Pallas kernels, fused(): pl.pallas_call(functools.partial(kernel, n, columns), out_shape=pltpu.VME...  237 us

profile of v1, /device:TPU:9, one launch (start us, length us, event | category | flops | bytes accessed | tf_op | source)
XLA Modules:
  0.0 240.5 jit_solution(6431065959136293)
XLA Ops:
  0.0 237.1 %pair_exchange.1 = f32[1024,2048]{1,0:T(8,128)S(1)} custom-call(f32[1024,2048]{1,0:T(8,128)} %bitcast.5, f32[128,2048]{1,0:T(8,128)} %bitcast.6, f32[1,64]{1,0:T(1,128)} %bitcast.7, f32[16]{0:T(128)} %occ_i_ref.1, f32[2]{0:T(128)} %occ_j_ref.1), custom_call_target="tpu_custom_call" | custom-call | tf_op jit(solution)/shard_map/pair_exchange/pallas_call | solution.py:350
  237.1 3.4 %copy.7 = f32[16,64,2048]{2,1,0:T(8,128)} copy(f32[16,64,2048]{2,1,0:T(8,128)S(1)} %bitcast.4) | data formatting | bytes 16777216

commit v2 on v1

--- a/solution.py
+++ b/solution.py
@@ -18,8 +18,8 @@
 
 
 def kernel(
-    n, columns, i_ref, j_ref, energy_ref, occ_i_ref, occ_j_ref, total,
-    i_high, i_low, j_all, direct, x_send, x_recv, j_parts, amp_parts, row_ref,
+    n, columns, i_ref, j_ref, energy_in, occ_i_in, occ_j_in, total, amp_parts, j_parts,
+    i_high, i_low, j_all, direct, x_send, x_recv, row_ref, energy_ref, occ_i_ref, occ_j_ref,
     local_sem, j_send_sem, j_recv_sem, x_send_sem, x_recv_sem,
 ):
     levels = n // 2 // columns
@@ -32,11 +32,12 @@
     pair = 2 * LANES
     tall = 256
     chunks = rows // tall
-
-    load_i = pltpu.make_async_copy(i_ref, total, local_sem.at[0])
-    load_i.start()
+    halves = 2
+    wide = 512
+
     load_j = pltpu.make_async_copy(j_ref, j_all.at[me], local_sem.at[1])
     load_j.start()
+    load_i = pltpu.make_async_copy(i_ref, total, local_sem.at[0])
 
     barrier = pltpu.get_barrier_semaphore()
 
@@ -55,20 +56,30 @@
     def _():
         greet(me - 2 * columns)
 
-    inner = jnp.logical_and(z > 0, z + 1 < levels).astype(jnp.int32)
-    pl.semaphore_wait(barrier, columns + (inner + 1 if levels > 1 else 0))
-
-    def j_copy(origin, way, device):
+    inner = jnp.logical_and(z > 0, z + 1 < levels)
+    load_i.start()
+    small = [
+        pltpu.make_async_copy(source, target, local_sem.at[3 + place])
+        for place, (source, target) in enumerate(
+            ((energy_in, energy_ref), (occ_i_in, occ_i_ref), (occ_j_in, occ_j_ref))
+        )
+    ]
+    for copy in small:
+        copy.start()
+    pl.semaphore_wait(barrier, columns + (inner.astype(jnp.int32) + 1 if levels > 1 else 0))
+
+    def j_copy(origin, half, flow, device):
+        part = pl.ds(half * (LANES // halves), LANES // halves)
         return pltpu.make_async_remote_copy(
-            src_ref=j_all.at[origin],
-            dst_ref=j_all.at[origin],
-            send_sem=j_send_sem.at[origin, way],
-            recv_sem=j_recv_sem.at[origin],
+            src_ref=j_all.at[origin, part],
+            dst_ref=j_all.at[origin, part],
+            send_sem=j_send_sem.at[flow],
+            recv_sem=j_recv_sem.at[origin, half],
             device_id={"virt": device},
             device_id_type=MESH,
         )
 
-    def j_targets(origin, act):
+    def j_send(origin, half):
         place = origin // 2
         same_core = lax.rem(origin, 2) == core
         in_column = jnp.logical_and(same_core, lax.rem(place, columns) == y)
@@ -76,20 +87,37 @@
 
         @pl.when(jnp.logical_and(in_column, jnp.logical_and(z >= from_z, z + 1 < levels)))
         def _():
-            act(j_copy(origin, 0, me + 2 * columns))
+            j_copy(origin, half, 0, me + 2 * columns).start()
 
         @pl.when(jnp.logical_and(in_column, jnp.logical_and(z <= from_z, z > 0)))
         def _():
-            act(j_copy(origin, 1, me - 2 * columns))
+            j_copy(origin, half, 0, me - 2 * columns).start()
 
         if columns == 2:
             @pl.when(in_column)
             def _():
-                act(j_copy(origin, 2, me + 2 * (1 - 2 * y)))
+                j_copy(origin, half, 1, me + 2 * (1 - 2 * y)).start()
 
         @pl.when(same_core)
         def _():
-            act(j_copy(origin, 3, me + 1 - 2 * core))
+            j_copy(origin, half, 1, me + 1 - 2 * core).start()
+
+    def drain(sent, sem):
+        pltpu.make_async_remote_copy(
+            src_ref=sent, dst_ref=sent, send_sem=sem, recv_sem=sem,
+            device_id={"virt": me}, device_id_type=MESH,
+        ).wait_send()
+
+    def inward(at_z):
+        return jnp.where(2 * at_z >= levels, -1, 1)
+
+    def last_of(place):
+        at_z, at_y = place // columns, lax.rem(place, columns)
+        if columns == 2:
+            offset = 1 if levels > 1 else 0
+        else:
+            offset = jnp.maximum(at_z, levels - 1 - at_z)
+        return (at_z + inward(at_z) * offset) * columns + columns - 1 - at_y
 
     def x_rows(chunk):
         return pl.ds(pl.multiple_of(chunk * tall, tall), tall)
@@ -98,23 +126,26 @@
         return pltpu.make_async_remote_copy(
             src_ref=x_send.at[other, part],
             dst_ref=x_recv.at[origin, part],
-            send_sem=x_send_sem.at[other, slot],
-            recv_sem=x_recv_sem.at[origin, slot],
+            send_sem=x_send_sem.at[0],
+            recv_sem=x_recv_sem.at[slot],
             device_id={"virt": other},
             device_id_type=MESH,
         )
 
-    def x_block(other, origin, chunk):
-        return x_copy(other, origin, x_rows(chunk), chunk)
+    def x_block(other, chunk):
+        late = last_of(other // 2) == chip
+        slot = jnp.where(late, n + core * chunks + chunk, me)
+        return x_copy(other, me, x_rows(chunk), slot)
 
     def x_energy(other, origin):
-        return x_copy(other, origin, pl.ds(rows, 1), chunks)
+        return x_copy(other, origin, pl.ds(rows, 1), origin)
 
     def x_stay():
         return pltpu.make_async_copy(x_send.at[me], x_recv.at[me], local_sem.at[2])
 
     load_j.wait()
-    j_targets(me, lambda copy: copy.start())
+    for half in range(halves):
+        j_send(me, half)
     load_i.wait()
 
     @pl.loop(0, rows // 32)
@@ -125,6 +156,8 @@
         i_low[part, :] = low
         total[part, :] = jnp.zeros((32, depth), jnp.float32)
 
+    for copy in small:
+        copy.wait()
     width = energy_ref.shape[1]
     energy = energy_ref[...]
     twice = jnp.concatenate([energy, energy], axis=1)
@@ -153,26 +186,28 @@
             if copies == 3:
                 j_parts[pl.ds(2 * pair + base, 32), :] = high
 
-    toward = jnp.where(2 * z >= levels, -1, 1)
+    toward = inward(z)
+    deepest = jnp.maximum(z, levels - 1 - z)
+    beside = 2 * levels
+    visits = beside + (columns - 1) * levels
 
     def visit(step):
-        level = step // 4
-        kind = lax.rem(step // 2, 2)
-        sign = lax.rem(step, 2)
-        distance = level - kind
-        at_y = jnp.where(kind == 0, y, columns - 1 - y)
+        crossed = step >= beside
+        turn = step - beside
+        depth_in = jnp.where(turn < deepest - 1, deepest - turn, deepest - 1 - turn)
+        if levels > 1:
+            depth_in = jnp.where(turn == levels - 1, 1, depth_in)
+        distance = step // 2
 
         def on(way):
-            at_z = z + toward * (1 - 2 * way) * distance
-            valid = jnp.logical_and(distance >= 0, jnp.logical_and(at_z >= 0, at_z < levels))
-            valid = jnp.logical_and(valid, jnp.logical_or(distance > 0, way == 0))
-            if columns == 1:
-                valid = jnp.logical_and(valid, kind == 0)
-            return valid, at_z * columns + at_y
-
-        return on, sign
-
-    visits = 4 * (levels + columns - 1)
+            offset = jnp.where(crossed, depth_in, (1 - 2 * way) * distance)
+            at_z = z + toward * offset
+            valid = jnp.logical_and(at_z >= 0, at_z < levels)
+            once = jnp.logical_or(way == 0, jnp.logical_and(step < beside, distance > 0))
+            at_y = jnp.where(crossed, columns - 1 - y, y)
+            return jnp.logical_and(valid, once), at_z * columns + at_y
+
+        return on, jnp.where(crossed, 0, lax.rem(step, 2))
 
     @pl.loop(0, visits)
     def _(step):
@@ -186,14 +221,16 @@
 
                 @pl.when(jnp.logical_and(valid, origin != me))
                 def _():
-                    j_copy(origin, 0, me).wait_recv()
-                    j_targets(origin, lambda copy: copy.start())
+                    for half in range(halves):
+                        j_copy(origin, half, 0, me).wait_recv()
+                        j_send(origin, half)
 
         valid, place = on(sign)
 
         @pl.when(valid)
         def _():
-            j_copy(2 * place + 1 - core, 0, me).wait_recv()
+            for half in range(halves):
+                j_copy(2 * place + 1 - core, half, 0, me).wait_recv()
             for side in range(2):
                 other = 2 * place + side
 
@@ -234,7 +271,7 @@
 
                     @pl.when(other != me)
                     def _():
-                        x_block(other, me, block).start()
+                        x_block(other, block).start()
 
             for side in range(2):
                 other = 2 * place + side
@@ -243,25 +280,22 @@
                 def _():
                     x_stay().start()
 
-    def await_energies(place):
+    def await_place(place):
         for side in range(2):
             other = 2 * place + side
 
             @pl.when(other != me)
             def _():
-                x_energy(other, other).wait_recv()
+                x_copy(other, other, pl.ds(0, rows + 1), other).wait_recv()
 
             @pl.when(other == me)
             def _():
                 x_stay().wait()
 
-    def await_blocks(place, chunk):
+    def await_late(chunk):
         for side in range(2):
-            other = 2 * place + side
-
-            @pl.when(other != me)
-            def _():
-                x_block(other, other, chunk).wait_recv()
+            other = 2 * last_place + side
+            x_copy(other, other, x_rows(chunk), n + side * chunks + chunk).wait_recv()
 
     def amplitudes(place, part):
         for side in range(2):
@@ -275,13 +309,7 @@
             amp_parts[part, pair + side * LANES:pair + (side + 1) * LANES] = high
             amp_parts[part, 2 * pair + side * LANES:2 * pair + (side + 1) * LANES] = low
 
-    farthest = jnp.maximum(z, levels - 1 - z)
-    if columns == 2 and levels > 1:
-        farthest = jnp.where(farthest == levels - 1, farthest - 1, farthest)
-    back = z - toward * farthest
-    forth = z + toward * farthest
-    back_valid = jnp.logical_and(back >= 0, back < levels)
-    last_place = jnp.where(back_valid, back, forth) * columns + columns - 1 - y
+    last_place = last_of(chip)
 
     @pl.loop(0, visits)
     def _(step):
@@ -291,11 +319,10 @@
         @pl.when(jnp.logical_and(valid, place != last_place))
         def _():
             split_j(place, 3)
-            await_energies(place)
+            await_place(place)
 
             @pl.loop(0, chunks)
             def _(block):
-                await_blocks(place, block)
                 amplitudes(place, x_rows(block))
 
             @pl.loop(0, depth // pair)
@@ -307,34 +334,65 @@
 
     split_j(last_place, 3)
 
-    @pl.loop(0, n)
-    def _(other):
-        j_targets(other, lambda copy: copy.wait_send())
-
-    await_energies(last_place)
+    def j_sent(flow, blocks):
+        drain(j_all.at[pl.ds(0, blocks)], j_send_sem.at[flow])
+
+    j_sent(1, n // 2 + (levels if columns == 2 else 0))
+    if levels > 1:
+        pl.when(inner)(lambda: j_sent(0, levels + 1))
+        pl.when(jnp.logical_not(inner))(lambda: j_sent(0, 1))
+
+    for side in range(2):
+        x_energy(2 * last_place + side, 2 * last_place + side).wait_recv()
 
     @pl.loop(0, chunks)
     def _(block):
         part = x_rows(block)
-        await_blocks(last_place, block)
+        await_late(block)
         amplitudes(last_place, part)
 
-        @pl.loop(0, depth // pair)
-        def _(strip):
-            at = pl.ds(pl.multiple_of(strip * pair, pair), pair)
-            total[part, at] += jnp.dot(
-                amp_parts[part, :], j_parts[:, at], preferred_element_type=jnp.float32
-            )
-
-    @pl.loop(0, n)
-    def _(other):
-        @pl.when(other != me)
-        def _():
-            x_energy(other, me).wait_send()
-
-            @pl.loop(0, chunks)
-            def _(chunk):
-                x_block(other, me, chunk).wait_send()
+        @pl.when(block < chunks - 1)
+        def _():
+            @pl.loop(0, depth // wide)
+            def _(strip):
+                at = pl.ds(pl.multiple_of(strip * wide, wide), wide)
+                total[part, at] += jnp.dot(
+                    amp_parts[part, :], j_parts[:, at], preferred_element_type=jnp.float32
+                )
+
+    drain(x_send.at[pl.ds(0, n - 1), pl.ds(0, rows + 1)], x_send_sem.at[0])
+
+
+def finish(total_ref, amp_ref, j_ref, out_ref, last_ref, sems):
+    rows, depth = total_ref.shape
+    tall = last_ref.shape[0]
+    ready = rows // tall - 1
+    strips = sems.shape[0] - ready
+    wide = depth // strips
+
+    def store(piece):
+        part = pl.ds(piece * tall, tall)
+        return pltpu.make_async_copy(total_ref.at[part], out_ref.at[part], sems.at[piece])
+
+    def store_last(strip):
+        at = pl.ds(strip * wide, wide)
+        return pltpu.make_async_copy(
+            last_ref.at[:, at], out_ref.at[pl.ds(ready * tall, tall), at], sems.at[ready + strip]
+        )
+
+    for piece in range(ready):
+        store(piece).start()
+    part = slice(ready * tall, rows)
+    for strip in range(strips):
+        at = slice(strip * wide, (strip + 1) * wide)
+        last_ref[:, at] = total_ref[part, at] + jnp.dot(
+            amp_ref[part, :], j_ref[:, at], preferred_element_type=jnp.float32
+        )
+        store_last(strip).start()
+    for piece in range(ready):
+        store(piece).wait()
+    for strip in range(strips):
+        store_last(strip).wait()
 
 
 def fused(columns, i_factors, j_factors, occ_i, occ_j, virt_energy):
@@ -346,12 +404,16 @@
     vmem = pl.BlockSpec(memory_space=pltpu.VMEM)
     f32, bf16 = jnp.float32, jnp.bfloat16
     dma = pltpu.SemaphoreType.DMA
-    smem = pl.BlockSpec(memory_space=pltpu.SMEM)
-    total = pl.pallas_call(
+    smem = pltpu.SMEM
+    held = pl.pallas_call(
         functools.partial(kernel, n, columns),
-        out_shape=pltpu.VMEM((rows, depth), f32),
-        in_specs=[anywhere, anywhere, vmem, smem, smem],
-        out_specs=vmem,
+        out_shape=(
+            pltpu.VMEM((rows, depth), f32),
+            pltpu.VMEM((rows, 6 * LANES), bf16),
+            pltpu.VMEM((6 * LANES, depth), bf16),
+        ),
+        in_specs=[anywhere] * 5,
+        out_specs=(vmem, vmem, vmem),
         scratch_shapes=[
             pltpu.VMEM((rows, depth), bf16),
             pltpu.VMEM((rows, depth), bf16),
@@ -359,24 +421,36 @@
             pltpu.VMEM((n // 2, rows, 2 * LANES), f32),
             pltpu.VMEM((n, rows + 8, LANES), f32),
             pltpu.VMEM((n, rows + 8, LANES), f32),
-            pltpu.VMEM((6 * LANES, depth), bf16),
-            pltpu.VMEM((rows, 6 * LANES), bf16),
             pltpu.VMEM((rows, LANES), f32),
-            dma((3,)),
-            dma((n, 4)),
-            dma((n,)),
-            dma((n, rows // 256 + 1)),
-            dma((n, rows // 256 + 1)),
+            pltpu.VMEM((1, width), f32),
+            smem((ni,), f32),
+            smem((nj,), f32),
+            dma((6,)),
+            dma((2,)),
+            dma((n, 2)),
+            dma((1,)),
+            dma((n + 2 * (rows // 256),)),
         ],
         compiler_params=pltpu.CompilerParams(
-            collective_id=0, has_side_effects=True, vmem_limit_bytes=55 * 2**20
+            collective_id=0, has_side_effects=True, vmem_limit_bytes=50 * 2**20
         ),
         name="pair_exchange",
     )(
         i_factors.reshape(rows, depth), j_factors.reshape(nj * width, depth),
         virt_energy.reshape(1, width), occ_i, occ_j,
     )
-    return total.reshape(i_factors.shape)
+    tall = 256
+    strips = 8
+    out = pl.pallas_call(
+        finish,
+        out_shape=jax.ShapeDtypeStruct((rows, depth), f32),
+        in_specs=[vmem, vmem, vmem],
+        out_specs=anywhere,
+        scratch_shapes=[pltpu.VMEM((tall, depth), f32), dma((rows // tall - 1 + strips,))],
+        compiler_params=pltpu.CompilerParams(vmem_limit_bytes=4 * 2**20),
+        name="store",
+    )(*[pltpu.with_memory_space_constraint(array, pltpu.VMEM) for array in held])
+    return out.reshape(i_factors.shape)
 
 
 def transpose_blocks(pair_block, blocks):

time: 245 us -> 234 us (0.955); the launches traced: 241 us -> 234 us
  local copies, waits for them, and re-layouts: 3.4 us -> 0 us
  Pallas kernels: 237 us -> 234 us
    unnamed x1 -> x0, local copies, waits for them, and re-layouts: 3.4 us -> none
    pallas_call x1 -> x2, Pallas kernels: 237 us -> 234 us  [the longest x1 230 us: fused(): pl.pallas_call(functools.partial(kernel, n, columns), out_shape=(pltpu.VM...]
where the time goes in v2:
time: 234 us
  Pallas kernels  234 us (100%)
    pallas_call x1, Pallas kernels, fused(): pl.pallas_call(functools.partial(kernel, n, columns), out_shape=(pltpu.VM...  230 us

profile of v2, /device:TPU:9, one launch (start us, length us, event | category | flops | bytes accessed | tf_op | source)
XLA Modules:
  0.0 233.8 jit_solution(17995920952266733956)
XLA Ops:
  0.0 230.4 %pair_exchange.1 = (f32[1024,2048]{1,0:T(8,128)S(1)}, bf16[1024,768]{1,0:T(8,128)(2,1)S(1)}, bf16[768,2048]{1,0:T(8,128)(2,1)S(1)}) custom-call(f32[1024,2048]{1,0:T(8,128)} %bitcast.4, f32[128,2048]{1,0:T(8,128)} %bitcast.5, f32[1,64]{1,0:T(1,128)} %bitcast.6, f32[16]{0:T(128)} %occ_i_in.1, f32[2]{0:T(128)} %occ_j_in.1), custom_call_target="tpu_custom_call" | custom-call | tf_op jit(solution)/shard_map/pair_exchange/pallas_call | solution.py:408
  230.4 3.4 %store.1 = f32[1024,2048]{1,0:T(8,128)} custom-call(f32[1024,2048]{1,0:T(8,128)S(1)} %get-tuple-element.8.total_ref, bf16[1024,768]{1,0:T(8,128)(2,1)S(1)} %get-tuple-element.9.amp_ref, bf16[768,2048]{1,0:T(8,128)(2,1)S(1)} %get-tuple-element.10.j_ref), custom_call_target="tpu_custom_call" | custom-call | tf_op jit(solution)/shard_map/store/pallas_call | solution.py:444

commit v3 on v2

--- a/solution.py
+++ b/solution.py
@@ -18,10 +18,11 @@
 
 
 def kernel(
-    n, columns, i_ref, j_ref, energy_in, occ_i_in, occ_j_in, total, amp_parts, j_parts,
+    n, i_ref, j_ref, energy_in, occ_i_in, occ_j_in, total, amp_parts, j_parts,
     i_high, i_low, j_all, direct, x_send, x_recv, row_ref, energy_ref, occ_i_ref, occ_j_ref,
     local_sem, j_send_sem, j_recv_sem, x_send_sem, x_recv_sem,
 ):
+    columns = 2
     levels = n // 2 // columns
     me = lax.axis_index("virt")
     core = lax.rem(me, 2)
@@ -45,8 +46,7 @@
         pl.semaphore_signal(barrier, inc=1, device_id={"virt": device}, device_id_type=MESH)
 
     greet(me + 1 - 2 * core)
-    if columns == 2:
-        greet(me + 2 * (1 - 2 * y))
+    greet(me + 2 * (1 - 2 * y))
 
     @pl.when(z + 1 < levels)
     def _():
@@ -66,18 +66,27 @@
     ]
     for copy in small:
         copy.start()
-    pl.semaphore_wait(barrier, columns + (inner.astype(jnp.int32) + 1 if levels > 1 else 0))
+    pl.semaphore_wait(barrier, 3 + inner.astype(jnp.int32))
 
     def j_copy(origin, half, flow, device):
         part = pl.ds(half * (LANES // halves), LANES // halves)
+        ahead = flow == 0 and half == 0
+        slot = n + origin // 2 // columns if ahead else origin
         return pltpu.make_async_remote_copy(
             src_ref=j_all.at[origin, part],
             dst_ref=j_all.at[origin, part],
             send_sem=j_send_sem.at[flow],
-            recv_sem=j_recv_sem.at[origin, half],
+            recv_sem=j_recv_sem.at[slot],
             device_id={"virt": device},
             device_id_type=MESH,
         )
+
+    def j_await(origin):
+        whole = j_all.at[origin]
+        pltpu.make_async_remote_copy(
+            src_ref=whole, dst_ref=whole, send_sem=j_send_sem.at[1], recv_sem=j_recv_sem.at[origin],
+            device_id={"virt": me}, device_id_type=MESH,
+        ).wait_recv()
 
     def j_send(origin, half):
         place = origin // 2
@@ -93,10 +102,9 @@
         def _():
             j_copy(origin, half, 0, me - 2 * columns).start()
 
-        if columns == 2:
-            @pl.when(in_column)
-            def _():
-                j_copy(origin, half, 1, me + 2 * (1 - 2 * y)).start()
+        @pl.when(in_column)
+        def _():
+            j_copy(origin, half, 1, me + 2 * (1 - 2 * y)).start()
 
         @pl.when(same_core)
         def _():
@@ -111,13 +119,11 @@
     def inward(at_z):
         return jnp.where(2 * at_z >= levels, -1, 1)
 
-    def last_of(place):
-        at_z, at_y = place // columns, lax.rem(place, columns)
-        if columns == 2:
-            offset = 1 if levels > 1 else 0
-        else:
-            offset = jnp.maximum(at_z, levels - 1 - at_z)
-        return (at_z + inward(at_z) * offset) * columns + columns - 1 - at_y
+    def ahead_of(place):
+        return place + inward(place // columns) * columns
+
+    def across(place):
+        return place + 1 - 2 * lax.rem(place, columns)
 
     def x_rows(chunk):
         return pl.ds(pl.multiple_of(chunk * tall, tall), tall)
@@ -133,12 +139,24 @@
         )
 
     def x_block(other, chunk):
-        late = last_of(other // 2) == chip
-        slot = jnp.where(late, n + core * chunks + chunk, me)
+        late = across(ahead_of(other // 2)) == chip
+        slot = jnp.where(late, n // 2 + core * chunks + chunk, chip)
         return x_copy(other, me, x_rows(chunk), slot)
 
-    def x_energy(other, origin):
-        return x_copy(other, origin, pl.ds(rows, 1), origin)
+    def x_held(other, origin):
+        return x_copy(
+            other, origin, x_rows(chunks - 1), n // 2 + 2 * chunks + lax.rem(origin, 2)
+        )
+
+    def x_energy(other):
+        return x_copy(other, me, pl.ds(rows, 1), chip)
+
+    def x_await(place, first, sides, count):
+        block = x_recv.at[pl.ds(first, sides), pl.ds(0, count)]
+        pltpu.make_async_remote_copy(
+            src_ref=block, dst_ref=block, send_sem=x_send_sem.at[0], recv_sem=x_recv_sem.at[place],
+            device_id={"virt": me}, device_id_type=MESH,
+        ).wait_recv()
 
     def x_stay():
         return pltpu.make_async_copy(x_send.at[me], x_recv.at[me], local_sem.at[2])
@@ -189,14 +207,13 @@
     toward = inward(z)
     deepest = jnp.maximum(z, levels - 1 - z)
     beside = 2 * levels
-    visits = beside + (columns - 1) * levels
+    visits = beside + levels
 
     def visit(step):
         crossed = step >= beside
         turn = step - beside
         depth_in = jnp.where(turn < deepest - 1, deepest - turn, deepest - 1 - turn)
-        if levels > 1:
-            depth_in = jnp.where(turn == levels - 1, 1, depth_in)
+        depth_in = jnp.where(turn == levels - 1, 1, depth_in)
         distance = step // 2
 
         def on(way):
@@ -219,24 +236,32 @@
                 valid, place = on(way)
                 origin = 2 * place + core
 
-                @pl.when(jnp.logical_and(valid, origin != me))
+                @pl.when(jnp.logical_and(jnp.logical_and(valid, step < beside), origin != me))
                 def _():
                     for half in range(halves):
                         j_copy(origin, half, 0, me).wait_recv()
                         j_send(origin, half)
 
+            _, place = on(0)
+            origin = 2 * place + core
+
+            @pl.when(step >= beside)
+            def _():
+                j_await(origin)
+                for half in range(halves):
+                    j_send(origin, half)
+
         valid, place = on(sign)
 
         @pl.when(valid)
         def _():
-            for half in range(halves):
-                j_copy(2 * place + 1 - core, half, 0, me).wait_recv()
+            j_await(2 * place + 1 - core)
             for side in range(2):
                 other = 2 * place + side
 
                 @pl.when(other != me)
                 def _():
-                    x_energy(other, me).start()
+                    x_energy(other).start()
 
             split_j(place, 2)
             lane = lax.broadcasted_iota(jnp.int32, (LANES // 2, LANES), 1)
@@ -266,10 +291,11 @@
                         base = start + group * LANES
                         x_send[2 * place + side, pl.ds(base, half), :] = first
                         x_send[2 * place + side, pl.ds(base + half, half), :] = second
+                hold = jnp.logical_and(ahead_of(place) == chip, block == chunks - 1)
                 for side in range(2):
                     other = 2 * place + side
 
-                    @pl.when(other != me)
+                    @pl.when(jnp.logical_and(other != me, jnp.logical_not(hold)))
                     def _():
                         x_block(other, block).start()
 
@@ -280,22 +306,36 @@
                 def _():
                     x_stay().start()
 
+    for way in (-1, 1):
+        place = chip + way * columns
+        there = jnp.logical_and(z + way >= 0, z + way < levels)
+
+        @pl.when(jnp.logical_and(there, ahead_of(place) == chip))
+        def _():
+            for side in range(2):
+                x_held(2 * place + side, me).start()
+
+    last_place = ahead_of(chip)
+    late_place = across(last_place)
+
     def await_place(place):
-        for side in range(2):
-            other = 2 * place + side
-
-            @pl.when(other != me)
-            def _():
-                x_copy(other, other, pl.ds(0, rows + 1), other).wait_recv()
-
-            @pl.when(other == me)
-            def _():
-                x_stay().wait()
+        @pl.when(place == chip)
+        def _():
+            x_await(chip, me + 1 - 2 * core, 1, rows + 1)
+            x_stay().wait()
+
+        @pl.when(place == last_place)
+        def _():
+            x_await(place, 2 * place, 2, rows - tall + 1)
+
+        @pl.when(jnp.logical_and(place != chip, place != last_place))
+        def _():
+            x_await(place, 2 * place, 2, rows + 1)
 
     def await_late(chunk):
         for side in range(2):
-            other = 2 * last_place + side
-            x_copy(other, other, x_rows(chunk), n + side * chunks + chunk).wait_recv()
+            other = 2 * late_place + side
+            x_copy(other, other, x_rows(chunk), n // 2 + side * chunks + chunk).wait_recv()
 
     def amplitudes(place, part):
         for side in range(2):
@@ -309,21 +349,24 @@
             amp_parts[part, pair + side * LANES:pair + (side + 1) * LANES] = high
             amp_parts[part, 2 * pair + side * LANES:2 * pair + (side + 1) * LANES] = low
 
-    last_place = last_of(chip)
-
     @pl.loop(0, visits)
     def _(step):
         on, sign = visit(step)
         valid, place = on(sign)
 
-        @pl.when(jnp.logical_and(valid, place != last_place))
+        @pl.when(jnp.logical_and(valid, place != late_place))
         def _():
             split_j(place, 3)
             await_place(place)
-
-            @pl.loop(0, chunks)
+            arrived = jnp.where(place == last_place, chunks - 1, chunks)
+
+            @pl.loop(0, arrived)
             def _(block):
                 amplitudes(place, x_rows(block))
+
+            @pl.when(place == last_place)
+            def _():
+                amp_parts[rows - tall:, :] = jnp.zeros((tall, 3 * pair), jnp.bfloat16)
 
             @pl.loop(0, depth // pair)
             def _(strip):
@@ -332,34 +375,33 @@
                     amp_parts[...], j_parts[:, at], preferred_element_type=jnp.float32
                 )
 
-    split_j(last_place, 3)
+    split_j(late_place, 3)
 
     def j_sent(flow, blocks):
         drain(j_all.at[pl.ds(0, blocks)], j_send_sem.at[flow])
 
-    j_sent(1, n // 2 + (levels if columns == 2 else 0))
-    if levels > 1:
-        pl.when(inner)(lambda: j_sent(0, levels + 1))
-        pl.when(jnp.logical_not(inner))(lambda: j_sent(0, 1))
-
-    for side in range(2):
-        x_energy(2 * last_place + side, 2 * last_place + side).wait_recv()
+    j_sent(1, n // 2 + levels)
+    pl.when(inner)(lambda: j_sent(0, levels + 1))
+    pl.when(jnp.logical_not(inner))(lambda: j_sent(0, 1))
+    x_await(late_place, 2 * late_place, 2, 1)
 
     @pl.loop(0, chunks)
     def _(block):
         part = x_rows(block)
         await_late(block)
-        amplitudes(last_place, part)
-
-        @pl.when(block < chunks - 1)
-        def _():
-            @pl.loop(0, depth // wide)
-            def _(strip):
-                at = pl.ds(pl.multiple_of(strip * wide, wide), wide)
-                total[part, at] += jnp.dot(
-                    amp_parts[part, :], j_parts[:, at], preferred_element_type=jnp.float32
-                )
-
+        amplitudes(late_place, part)
+
+        @pl.loop(0, depth // wide)
+        def _(strip):
+            at = pl.ds(pl.multiple_of(strip * wide, wide), wide)
+            total[part, at] += jnp.dot(
+                amp_parts[part, :], j_parts[:, at], preferred_element_type=jnp.float32
+            )
+
+    split_j(last_place, 3)
+    for side in range(2):
+        x_held(2 * last_place + side, 2 * last_place + side).wait_recv()
+    amplitudes(last_place, slice(rows - tall, rows))
     drain(x_send.at[pl.ds(0, n - 1), pl.ds(0, rows + 1)], x_send_sem.at[0])
 
 
@@ -395,7 +437,7 @@
         store_last(strip).wait()
 
 
-def fused(columns, i_factors, j_factors, occ_i, occ_j, virt_energy):
+def fused(i_factors, j_factors, occ_i, occ_j, virt_energy):
     n = lax.axis_size("virt")
     ni, width, depth = i_factors.shape
     nj = j_factors.shape[0]
@@ -406,7 +448,7 @@
     dma = pltpu.SemaphoreType.DMA
     smem = pltpu.SMEM
     held = pl.pallas_call(
-        functools.partial(kernel, n, columns),
+        functools.partial(kernel, n),
         out_shape=(
             pltpu.VMEM((rows, depth), f32),
             pltpu.VMEM((rows, 6 * LANES), bf16),
@@ -427,9 +469,9 @@
             smem((nj,), f32),
             dma((6,)),
             dma((2,)),
-            dma((n, 2)),
+            dma((n + n // 4,)),
             dma((1,)),
-            dma((n + 2 * (rows // 256),)),
+            dma((n // 2 + 2 * (rows // 256) + 2,)),
         ],
         compiler_params=pltpu.CompilerParams(
             collective_id=0, has_side_effects=True, vmem_limit_bytes=50 * 2**20
@@ -502,9 +544,10 @@
     nj = j_factors.shape[0]
     fits = nj == 2 and nj * width == LANES and (ni * width) % 256 == 0 and depth % 512 == 0
     n = lax.axis_size("virt")
+    tall_enough = columns == 2 and n // 4 >= 2
     room = 4 * ni * width * depth * 2 + 4 * n * LANES * (depth + 3 * (ni * width + 8))
-    if columns and fits and room < 58 * 2**20:
-        return fused(columns, i_factors, j_factors, occ_i, occ_j, virt_energy)
+    if tall_enough and fits and room < 58 * 2**20:
+        return fused(i_factors, j_factors, occ_i, occ_j, virt_energy)
     return general(i_factors, j_factors, occ_i, occ_j, virt_energy)
 
 

time: 234 us -> 233 us (level)
  no operation moved by 1% of the time
where the time goes in v3:
time: 233 us
  Pallas kernels  233 us (100%)
    pallas_call x1, Pallas kernels, fused(): pl.pallas_call(functools.partial(kernel, n), out_shape=(pltpu.VMEM((rows,...  229 us

profile of v3, /device:TPU:9, one launch (start us, length us, event | category | flops | bytes accessed | tf_op | source)
XLA Modules:
  0.0 232.8 jit_solution(5215758137153997032)
XLA Ops:
  0.0 229.4 %pair_exchange.1 = (f32[1024,2048]{1,0:T(8,128)S(1)}, bf16[1024,768]{1,0:T(8,128)(2,1)S(1)}, bf16[768,2048]{1,0:T(8,128)(2,1)S(1)}) custom-call(f32[1024,2048]{1,0:T(8,128)} %bitcast.4, f32[128,2048]{1,0:T(8,128)} %bitcast.5, f32[1,64]{1,0:T(1,128)} %bitcast.6, f32[16]{0:T(128)} %occ_i_in.1, f32[2]{0:T(128)} %occ_j_in.1), custom_call_target="tpu_custom_call" | custom-call | tf_op jit(solution)/shard_map/pair_exchange/pallas_call | solution.py:450
  229.4 3.4 %store.1 = f32[1024,2048]{1,0:T(8,128)} custom-call(f32[1024,2048]{1,0:T(8,128)S(1)} %get-tuple-element.8.total_ref, bf16[1024,768]{1,0:T(8,128)(2,1)S(1)} %get-tuple-element.9.amp_ref, bf16[768,2048]{1,0:T(8,128)(2,1)S(1)} %get-tuple-element.10.j_ref), custom_call_target="tpu_custom_call" | custom-call | tf_op jit(solution)/shard_map/store/pallas_call | solution.py:486

commit v4 on v3

--- a/solution.py
+++ b/solution.py
@@ -140,21 +140,19 @@
 
     def x_block(other, chunk):
         late = across(ahead_of(other // 2)) == chip
-        slot = jnp.where(late, n // 2 + core * chunks + chunk, chip)
+        slot = jnp.where(late, n // 2 + chunk, chip)
         return x_copy(other, me, x_rows(chunk), slot)
 
-    def x_held(other, origin):
-        return x_copy(
-            other, origin, x_rows(chunks - 1), n // 2 + 2 * chunks + lax.rem(origin, 2)
-        )
+    def x_held(other):
+        return x_copy(other, me, x_rows(chunks - 1), n // 2 + chunks)
 
     def x_energy(other):
         return x_copy(other, me, pl.ds(rows, 1), chip)
 
-    def x_await(place, first, sides, count):
+    def x_await(slot, first, sides, count):
         block = x_recv.at[pl.ds(first, sides), pl.ds(0, count)]
         pltpu.make_async_remote_copy(
-            src_ref=block, dst_ref=block, send_sem=x_send_sem.at[0], recv_sem=x_recv_sem.at[place],
+            src_ref=block, dst_ref=block, send_sem=x_send_sem.at[0], recv_sem=x_recv_sem.at[slot],
             device_id={"virt": me}, device_id_type=MESH,
         ).wait_recv()
 
@@ -256,10 +254,11 @@
         @pl.when(valid)
         def _():
             j_await(2 * place + 1 - core)
+            pieces = jnp.logical_or(ahead_of(place) == chip, across(ahead_of(place)) == chip)
             for side in range(2):
                 other = 2 * place + side
 
-                @pl.when(other != me)
+                @pl.when(jnp.logical_and(other != me, pieces))
                 def _():
                     x_energy(other).start()
 
@@ -295,9 +294,17 @@
                 for side in range(2):
                     other = 2 * place + side
 
-                    @pl.when(jnp.logical_and(other != me, jnp.logical_not(hold)))
+                    by_piece = jnp.logical_and(pieces, jnp.logical_not(hold))
+
+                    @pl.when(jnp.logical_and(other != me, by_piece))
                     def _():
                         x_block(other, block).start()
+
+                    done = jnp.logical_and(jnp.logical_not(pieces), block == chunks - 1)
+
+                    @pl.when(jnp.logical_and(other != me, done))
+                    def _():
+                        x_copy(other, me, pl.ds(0, rows + 1), chip).start()
 
             for side in range(2):
                 other = 2 * place + side
@@ -313,7 +320,7 @@
         @pl.when(jnp.logical_and(there, ahead_of(place) == chip))
         def _():
             for side in range(2):
-                x_held(2 * place + side, me).start()
+                x_held(2 * place + side).start()
 
     last_place = ahead_of(chip)
     late_place = across(last_place)
@@ -331,11 +338,6 @@
         @pl.when(jnp.logical_and(place != chip, place != last_place))
         def _():
             x_await(place, 2 * place, 2, rows + 1)
-
-    def await_late(chunk):
-        for side in range(2):
-            other = 2 * late_place + side
-            x_copy(other, other, x_rows(chunk), n // 2 + side * chunks + chunk).wait_recv()
 
     def amplitudes(place, part):
         for side in range(2):
@@ -388,7 +390,7 @@
     @pl.loop(0, chunks)
     def _(block):
         part = x_rows(block)
-        await_late(block)
+        x_await(n // 2 + block, 2 * late_place, 2, tall)
         amplitudes(late_place, part)
 
         @pl.loop(0, depth // wide)
@@ -399,42 +401,31 @@
             )
 
     split_j(last_place, 3)
-    for side in range(2):
-        x_held(2 * last_place + side, 2 * last_place + side).wait_recv()
+    x_await(n // 2 + chunks, 2 * last_place, 2, tall)
     amplitudes(last_place, slice(rows - tall, rows))
     drain(x_send.at[pl.ds(0, n - 1), pl.ds(0, rows + 1)], x_send_sem.at[0])
 
 
-def finish(total_ref, amp_ref, j_ref, out_ref, last_ref, sems):
+def finish(total_ref, amp_ref, j_ref, out_ref, last_ref, sem):
     rows, depth = total_ref.shape
     tall = last_ref.shape[0]
-    ready = rows // tall - 1
-    strips = sems.shape[0] - ready
-    wide = depth // strips
-
-    def store(piece):
-        part = pl.ds(piece * tall, tall)
-        return pltpu.make_async_copy(total_ref.at[part], out_ref.at[part], sems.at[piece])
-
-    def store_last(strip):
-        at = pl.ds(strip * wide, wide)
-        return pltpu.make_async_copy(
-            last_ref.at[:, at], out_ref.at[pl.ds(ready * tall, tall), at], sems.at[ready + strip]
-        )
-
-    for piece in range(ready):
-        store(piece).start()
-    part = slice(ready * tall, rows)
-    for strip in range(strips):
-        at = slice(strip * wide, (strip + 1) * wide)
-        last_ref[:, at] = total_ref[part, at] + jnp.dot(
-            amp_ref[part, :], j_ref[:, at], preferred_element_type=jnp.float32
-        )
-        store_last(strip).start()
-    for piece in range(ready):
-        store(piece).wait()
-    for strip in range(strips):
-        store_last(strip).wait()
+    ready = rows - tall
+    wide = 256
+
+    for start in range(0, ready, tall):
+        part = pl.ds(start, tall)
+        pltpu.make_async_copy(total_ref.at[part], out_ref.at[part], sem.at[0]).start()
+    for start in range(0, depth, wide):
+        at = slice(start, start + wide)
+        last_ref[:, at] = total_ref[ready:, at] + jnp.dot(
+            amp_ref[ready:, :], j_ref[:, at], preferred_element_type=jnp.float32
+        )
+        pltpu.make_async_copy(
+            last_ref.at[:, pl.ds(start, wide)],
+            out_ref.at[pl.ds(ready, tall), pl.ds(start, wide)],
+            sem.at[0],
+        ).start()
+    pltpu.make_async_copy(total_ref, out_ref, sem.at[0]).wait()
 
 
 def fused(i_factors, j_factors, occ_i, occ_j, virt_energy):
@@ -471,7 +462,7 @@
             dma((2,)),
             dma((n + n // 4,)),
             dma((1,)),
-            dma((n // 2 + 2 * (rows // 256) + 2,)),
+            dma((n // 2 + rows // 256 + 1,)),
         ],
         compiler_params=pltpu.CompilerParams(
             collective_id=0, has_side_effects=True, vmem_limit_bytes=50 * 2**20
@@ -481,14 +472,12 @@
         i_factors.reshape(rows, depth), j_factors.reshape(nj * width, depth),
         virt_energy.reshape(1, width), occ_i, occ_j,
     )
-    tall = 256
-    strips = 8
     out = pl.pallas_call(
         finish,
         out_shape=jax.ShapeDtypeStruct((rows, depth), f32),
         in_specs=[vmem, vmem, vmem],
         out_specs=anywhere,
-        scratch_shapes=[pltpu.VMEM((tall, depth), f32), dma((rows // tall - 1 + strips,))],
+        scratch_shapes=[pltpu.VMEM((256, depth), f32), dma((1,))],
         compiler_params=pltpu.CompilerParams(vmem_limit_bytes=4 * 2**20),
         name="store",
     )(*[pltpu.with_memory_space_constraint(array, pltpu.VMEM) for array in held])

time: 233 us -> 233 us (level)
  no operation moved by 1% of the time
where the time goes in v4:
time: 233 us
  Pallas kernels  233 us (100%)
    pallas_call x1, Pallas kernels, fused(): pl.pallas_call(functools.partial(kernel, n), out_shape=(pltpu.VMEM((rows,...  229 us

profile of v4, /device:TPU:9, one launch (start us, length us, event | category | flops | bytes accessed | tf_op | source)
XLA Modules:
  0.0 232.6 jit_solution(13288804207823749435)
XLA Ops:
  0.0 229.3 %pair_exchange.1 = (f32[1024,2048]{1,0:T(8,128)S(1)}, bf16[1024,768]{1,0:T(8,128)(2,1)S(1)}, bf16[768,2048]{1,0:T(8,128)(2,1)S(1)}) custom-call(f32[1024,2048]{1,0:T(8,128)} %bitcast.4, f32[128,2048]{1,0:T(8,128)} %bitcast.5, f32[1,64]{1,0:T(1,128)} %bitcast.6, f32[16]{0:T(128)} %occ_i_in.1, f32[2]{0:T(128)} %occ_j_in.1), custom_call_target="tpu_custom_call" | custom-call | tf_op jit(solution)/shard_map/pair_exchange/pallas_call | solution.py:441
  229.4 3.3 %store.1 = f32[1024,2048]{1,0:T(8,128)} custom-call(f32[1024,2048]{1,0:T(8,128)S(1)} %get-tuple-element.8.total_ref, bf16[1024,768]{1,0:T(8,128)(2,1)S(1)} %get-tuple-element.9.amp_ref, bf16[768,2048]{1,0:T(8,128)(2,1)S(1)} %get-tuple-element.10.j_ref), custom_call_target="tpu_custom_call" | custom-call | tf_op jit(solution)/shard_map/store/pallas_call | solution.py:475

commit v5 on v3

--- a/solution.py
+++ b/solution.py
@@ -33,7 +33,7 @@
     pair = 2 * LANES
     tall = 256
     chunks = rows // tall
-    halves = 2
+    parts = 4
     wide = 512
 
     load_j = pltpu.make_async_copy(j_ref, j_all.at[me], local_sem.at[1])
@@ -68,10 +68,10 @@
         copy.start()
     pl.semaphore_wait(barrier, 3 + inner.astype(jnp.int32))
 
-    def j_copy(origin, half, flow, device):
-        part = pl.ds(half * (LANES // halves), LANES // halves)
-        ahead = flow == 0 and half == 0
-        slot = n + origin // 2 // columns if ahead else origin
+    def j_copy(origin, piece, flow, device):
+        part = pl.ds(piece * (LANES // parts), LANES // parts)
+        ahead = flow == 0 and piece < parts - 1
+        slot = n + piece * levels + origin // 2 // columns if ahead else origin
         return pltpu.make_async_remote_copy(
             src_ref=j_all.at[origin, part],
             dst_ref=j_all.at[origin, part],
@@ -88,7 +88,7 @@
             device_id={"virt": me}, device_id_type=MESH,
         ).wait_recv()
 
-    def j_send(origin, half):
+    def j_send(origin, piece):
         place = origin // 2
         same_core = lax.rem(origin, 2) == core
         in_column = jnp.logical_and(same_core, lax.rem(place, columns) == y)
@@ -96,19 +96,19 @@
 
         @pl.when(jnp.logical_and(in_column, jnp.logical_and(z >= from_z, z + 1 < levels)))
         def _():
-            j_copy(origin, half, 0, me + 2 * columns).start()
+            j_copy(origin, piece, 0, me + 2 * columns).start()
 
         @pl.when(jnp.logical_and(in_column, jnp.logical_and(z <= from_z, z > 0)))
         def _():
-            j_copy(origin, half, 0, me - 2 * columns).start()
+            j_copy(origin, piece, 0, me - 2 * columns).start()
 
         @pl.when(in_column)
         def _():
-            j_copy(origin, half, 1, me + 2 * (1 - 2 * y)).start()
+            j_copy(origin, piece, 1, me + 2 * (1 - 2 * y)).start()
 
         @pl.when(same_core)
         def _():
-            j_copy(origin, half, 1, me + 1 - 2 * core).start()
+            j_copy(origin, piece, 1, me + 1 - 2 * core).start()
 
     def drain(sent, sem):
         pltpu.make_async_remote_copy(
@@ -162,8 +162,8 @@
         return pltpu.make_async_copy(x_send.at[me], x_recv.at[me], local_sem.at[2])
 
     load_j.wait()
-    for half in range(halves):
-        j_send(me, half)
+    for piece in range(parts):
+        j_send(me, piece)
     load_i.wait()
 
     @pl.loop(0, rows // 32)
@@ -238,9 +238,9 @@
 
                 @pl.when(jnp.logical_and(jnp.logical_and(valid, step < beside), origin != me))
                 def _():
-                    for half in range(halves):
-                        j_copy(origin, half, 0, me).wait_recv()
-                        j_send(origin, half)
+                    for piece in range(parts):
+                        j_copy(origin, piece, 0, me).wait_recv()
+                        j_send(origin, piece)
 
             _, place = on(0)
             origin = 2 * place + core
@@ -248,8 +248,8 @@
             @pl.when(step >= beside)
             def _():
                 j_await(origin)
-                for half in range(halves):
-                    j_send(origin, half)
+                for piece in range(parts):
+                    j_send(origin, piece)
 
         valid, place = on(sign)
 
@@ -469,7 +469,7 @@
             smem((nj,), f32),
             dma((6,)),
             dma((2,)),
-            dma((n + n // 4,)),
+            dma((n + 3 * (n // 4),)),
             dma((1,)),
             dma((n // 2 + 2 * (rows // 256) + 2,)),
         ],

time: 233 us -> 233 us (level)
  no operation moved by 1% of the time
where the time goes in v5:
time: 233 us
  Pallas kernels  233 us (100%)
    pallas_call x1, Pallas kernels, fused(): pl.pallas_call(functools.partial(kernel, n), out_shape=(pltpu.VMEM((rows,...  229 us

profile of v5, /device:TPU:9, one launch (start us, length us, event | category | flops | bytes accessed | tf_op | source)
XLA Modules:
  0.0 232.8 jit_solution(2206898297270547300)
XLA Ops:
  0.0 229.5 %pair_exchange.1 = (f32[1024,2048]{1,0:T(8,128)S(1)}, bf16[1024,768]{1,0:T(8,128)(2,1)S(1)}, bf16[768,2048]{1,0:T(8,128)(2,1)S(1)}) custom-call(f32[1024,2048]{1,0:T(8,128)} %bitcast.4, f32[128,2048]{1,0:T(8,128)} %bitcast.5, f32[1,64]{1,0:T(1,128)} %bitcast.6, f32[16]{0:T(128)} %occ_i_in.1, f32[2]{0:T(128)} %occ_j_in.1), custom_call_target="tpu_custom_call" | custom-call | tf_op jit(solution)/shard_map/pair_exchange/pallas_call | solution.py:450
  229.5 3.4 %store.1 = f32[1024,2048]{1,0:T(8,128)} custom-call(f32[1024,2048]{1,0:T(8,128)S(1)} %get-tuple-element.8.total_ref, bf16[1024,768]{1,0:T(8,128)(2,1)S(1)} %get-tuple-element.9.amp_ref, bf16[768,2048]{1,0:T(8,128)(2,1)S(1)} %get-tuple-element.10.j_ref), custom_call_target="tpu_custom_call" | custom-call | tf_op jit(solution)/shard_map/store/pallas_call | solution.py:486

commit v6 on v3

--- a/solution.py
+++ b/solution.py
@@ -337,8 +337,8 @@
             other = 2 * late_place + side
             x_copy(other, other, x_rows(chunk), n // 2 + side * chunks + chunk).wait_recv()
 
-    def amplitudes(place, part):
-        for side in range(2):
+    def amplitudes(place, part, sides=(0, 1)):
+        for side in sides:
             other = 2 * place + side
             lanes = slice(side * LANES, (side + 1) * LANES)
             swapped = x_recv[other, part, :]
@@ -401,7 +401,7 @@
     split_j(last_place, 3)
     for side in range(2):
         x_held(2 * last_place + side, 2 * last_place + side).wait_recv()
-    amplitudes(last_place, slice(rows - tall, rows))
+        amplitudes(last_place, slice(rows - tall, rows), (side,))
     drain(x_send.at[pl.ds(0, n - 1), pl.ds(0, rows + 1)], x_send_sem.at[0])
 
 
@@ -482,7 +482,7 @@
         virt_energy.reshape(1, width), occ_i, occ_j,
     )
     tall = 256
-    strips = 8
+    strips = 4
     out = pl.pallas_call(
         finish,
         out_shape=jax.ShapeDtypeStruct((rows, depth), f32),

time: 233 us -> 233 us (level)
  no operation moved by 1% of the time
where the time goes in v6:
time: 233 us
  Pallas kernels  233 us (100%)
    pallas_call x1, Pallas kernels, fused(): pl.pallas_call(functools.partial(kernel, n), out_shape=(pltpu.VMEM((rows,...  229 us

profile of v6, /device:TPU:9, one launch (start us, length us, event | category | flops | bytes accessed | tf_op | source)
XLA Modules:
  0.0 232.7 jit_solution(9930955817139601971)
XLA Ops:
  0.0 229.4 %pair_exchange.1 = (f32[1024,2048]{1,0:T(8,128)S(1)}, bf16[1024,768]{1,0:T(8,128)(2,1)S(1)}, bf16[768,2048]{1,0:T(8,128)(2,1)S(1)}) custom-call(f32[1024,2048]{1,0:T(8,128)} %bitcast.4, f32[128,2048]{1,0:T(8,128)} %bitcast.5, f32[1,64]{1,0:T(1,128)} %bitcast.6, f32[16]{0:T(128)} %occ_i_in.1, f32[2]{0:T(128)} %occ_j_in.1), custom_call_target="tpu_custom_call" | custom-call | tf_op jit(solution)/shard_map/pair_exchange/pallas_call | solution.py:450
  229.4 3.3 %store.1 = f32[1024,2048]{1,0:T(8,128)} custom-call(f32[1024,2048]{1,0:T(8,128)S(1)} %get-tuple-element.8.total_ref, bf16[1024,768]{1,0:T(8,128)(2,1)S(1)} %get-tuple-element.9.amp_ref, bf16[768,2048]{1,0:T(8,128)(2,1)S(1)} %get-tuple-element.10.j_ref), custom_call_target="tpu_custom_call" | custom-call | tf_op jit(solution)/shard_map/store/pallas_call | solution.py:486
